TPU v7x, 32 devices: a whole 2x2x4 slice. The times are simulated.
32 devices in a mesh: depth: 4 (over z), row: 2 (over core), col: 4 (over y, x).
Axes of the slice: x: 2, y: 2, z: 4, core: 2. Of those that a mesh axis runs over, the one named last changes fastest.
Arguments:
- volume: bfloat16 [4, 18, 256, 8192], P('depth', None, 'row', 'col'), may hold values from -6 to 6
- order: int32 [4], replicated, may hold values from 0 to 3, each once
- empty: int32 [4, 2, 4], P('depth', 'row', 'col'), may hold values 0 or 1
- bump_center: float32 [4], replicated, may hold values from -1.5 to 1.5
- bump_width: float32 [4], replicated, may hold values from 0.3 to 1
- bump_height: float32 [4], replicated, may hold values from 0.5 to 4
- bump_color: float32 [3, 4], replicated, may hold values from 0.5 to 2
- light_dir: float32 [3], replicated, may hold values from -1 to 1
Outputs:
- image: float32 [2, 4, 128, 8192], P('row', None, 'depth', 'col')
Inputs may be any that keep to these rules, and one draw needn't show every extreme that they name: `order`: a permutation of the depth indices.
All inputs are finite; a program needn't handle non-finite values. No bound on the sum of `empty` on one device may be relied on, other than what follows from the above.
Results may differ from a plain program's by a relative error of at most 0.0003.
Values may be sent and summed in bfloat16 or wider, within the bound.
No kernel may reach another device: no remote copies, remote signals or barrier semaphores. Data moves between devices by JAX's collectives and lax.ppermute only.
A program may use at most 128 MiB of HBM per device.

v0:
```python
import jax
import jax.numpy as jnp
from jax import lax
from jax.sharding import PartitionSpec as P

slab_depth = 8
absorption = 0.08


def with_halo(x, sides, width):
    for axis, dim in sides:
        count, length = (lax.axis_size(axis), x.shape[dim])
        up = [(i, (i + 1) % count) for i in range(count - 1)]
        down = [(j, i) for i, j in up]
        last = lax.slice_in_dim(x, length - width, length, axis=dim)
        leading = lax.slice_in_dim(x, 0, width, axis=dim)
        before = lax.ppermute(last, axis, up)
        after = lax.ppermute(leading, axis, down)
        x = jnp.concatenate([before, x, after], axis=dim)
    return x


def march_brick(padded, bump_center, bump_width, bump_height, bump_color, light_dir):
    depth_len = padded.shape[0] - 2
    row_count = padded.shape[1] - 2
    col_count = padded.shape[2] - 2
    per_sample = absorption / depth_len

    def advance(state_pair, slab_index):
        through, radiance = state_pair
        block_cells = lax.dynamic_slice_in_dim(
            padded, slab_index * slab_depth, slab_depth + 2, 0
        ).astype(jnp.float32)
        samples = block_cells[1:-1, 1:-1, 1:-1]
        grad_z = 0.5 * (block_cells[2:, 1:-1, 1:-1] - block_cells[:-2, 1:-1, 1:-1])
        grad_y = 0.5 * (block_cells[1:-1, 2:, 1:-1] - block_cells[1:-1, :-2, 1:-1])
        grad_x = 0.5 * (block_cells[1:-1, 1:-1, 2:] - block_cells[1:-1, 1:-1, :-2])
        facing = jnp.abs(light_dir[0] * grad_z + light_dir[1] * grad_y + light_dir[2] * grad_x)
        shading = 0.3 + 0.7 * facing / jnp.sqrt(
            grad_z * grad_z + grad_y * grad_y + grad_x * grad_x + 1.0
        )
        density = jnp.zeros_like(samples)
        emission = [jnp.zeros_like(samples) for channel in range(3)]
        for bump_index in range(bump_center.shape[0]):
            offset = samples - bump_center[bump_index]
            bump_value = jnp.exp(
                -offset * offset / (2.0 * bump_width[bump_index] * bump_width[bump_index])
            )
            density = density + bump_height[bump_index] * bump_value
            emission = [
                emission[channel] + bump_color[channel, bump_index] * bump_value
                for channel in range(3)
            ]
        passing = jnp.exp(-per_sample * density)
        inclusive = jnp.cumprod(passing, axis=0)
        transmit = jnp.concatenate([jnp.ones_like(passing[:1]), inclusive[:-1]], 0) * through
        weights = transmit * (1.0 - passing) * shading
        radiance = radiance + jnp.stack(
            [jnp.sum(weights * emission[channel], 0) for channel in range(3)]
        )
        return ((through * inclusive[-1], radiance), None)

    start_carry = (
        jnp.ones((row_count, col_count), jnp.float32),
        jnp.zeros((3, row_count, col_count), jnp.float32),
    )
    (through, radiance), unused = lax.scan(
        advance, start_carry, jnp.arange(depth_len // slab_depth, dtype=jnp.int32)
    )
    return jnp.concatenate([radiance, (1.0 - through)[None]], 0)


def composite(stacked, order):
    ranked = jnp.take(stacked, order, axis=0)

    def layer_over(state_pair, layer_image):
        through, summed = state_pair
        summed = summed + through[None] * layer_image
        return ((through * (1.0 - layer_image[3]), summed), None)

    start_carry = (
        jnp.ones(stacked.shape[2:], jnp.float32),
        jnp.zeros(stacked.shape[1:], jnp.float32),
    )
    (through, summed), unused = lax.scan(layer_over, start_carry, ranked)
    return summed


def per_device(volume, order, empty, bump_center, bump_width, bump_height, bump_color, light_dir):
    padded = with_halo(volume[0], (("row", 1), ("col", 2)), 1)
    row_count = volume.shape[2]
    col_count = volume.shape[3]

    def blank_layer():
        return jnp.zeros((4, row_count, col_count), jnp.float32)

    def lit_layer():
        return march_brick(padded, bump_center, bump_width, bump_height, bump_color, light_dir)

    layer_image = lax.cond(empty[0, 0, 0] == 1, blank_layer, lit_layer)
    band_rows = composite(
        lax.all_to_all(layer_image[None], "depth", split_axis=2, concat_axis=0, tiled=True), order
    )
    return band_rows[None]


def solution(mesh):
    placed = (
        P("depth", None, "row", "col"),
        P(),
        P("depth", "row", "col"),
        P(),
        P(),
        P(),
        P(),
        P(),
    )
    return jax.shard_map(
        per_device,
        mesh=mesh,
        in_specs=placed,
        out_specs=P("row", None, "depth", "col"),
        check_vma=False,
    )
```

profile of v0, /device:TPU:5, one launch (start us, length us, event | category | flops | bytes accessed | tf_op | source)
XLA Modules:
  0.0 430.9 jit_solution(2655064788858189192)
XLA Ops:
  0.0 11.8 %copy.50 = bf16[1,18,128,2048]{3,1,2,0:T(8,128)(2,1)S(1)} copy(bf16[1,18,128,2048]{3,2,1,0:T(8,128)(2,1)} %param.14) | data formatting | bytes 18874368 | tf_op args[0]
  11.8 1.3 collective-permute-start
  13.1 3.0 collective-permute-start.1
  16.1 0.0 collective-permute-done
  16.1 0.9 collective-permute-done.1
  17.1 3.0 pad_maximum_fusion.1
  20.0 0.0 copy-start.2
  20.1 4.6 %copy-done.2 = bf16[18,130,2048]{2,0,1:T(8,128)(2,1)} copy-done((bf16[18,130,2048]{2,0,1:T(8,128)(2,1)}, bf16[18,130,2048]{2,0,1:T(8,128)(2,1)S(1)}, u32[]{:S(2)}) %copy-start.2) | copy-done | bytes 9584664
  24.6 0.4 fusion.18
  25.1 0.7 copy.37
  25.7 3.1 collective-permute-start.2
  28.9 0.7 copy.38
  29.5 3.1 collective-permute-start.3
  33.3 11.0 %copy.40 = bf16[18,130,2048]{2,1,0:T(8,128)(2,1)} copy(bf16[18,130,2048]{2,0,1:T(8,128)(2,1)} %copy-done.2) | data formatting | bytes 19169280 | tf_op jit(solution)/shard_map/concatenate | solution.py:19
  44.2 0.0 collective-permute-done.2
  44.3 0.4 copy.39
  44.6 0.0 collective-permute-done.3
  44.6 0.4 copy.41
  45.0 0.0 copy-start.7
  45.0 0.0 copy-start.8
  45.1 19.2 %concatenate.13 = bf16[18,130,2050]{2,1,0:T(8,128)(2,1)} concatenate(bf16[18,130,1]{2,1,0:T(8,128)(2,1)S(1)} %copy.39, bf16[18,130,2048]{2,1,0:T(8,128)(2,1)} %copy.40, bf16[18,130,1]{2,1,0:T(8,128)(2,1)S(1)} %copy.41), dimensions={2} | concatenate | bytes 19188000 | tf_op jit(solution)/shard_map/concatenate | solution.py:19
  64.3 0.0 copy-done.7
  64.3 0.0 copy-done.8
  64.3 2.5 conditional.1
  64.3 2.5 broadcast.64
  66.8 0.0 copy-start.9
  66.8 6.9 %copy.52 = f32[4,128,2048]{2,0,1:T(4,128)} copy(f32[4,128,2048]{2,1,0:T(8,128)} %get-tuple-element.623) | data formatting | bytes 8388608 | tf_op jit(solution)/shard_map/cond | solution.py:100
  73.6 234.6 %all-to-all-start = ((f32[1,4,128,2048]{3,1,0,2:T(4,128)}), f32[1,4,128,2048]{3,1,0,2:T(4,128)}, u32[]{:S(2)}, u32[]{:S(2)}) async-start(f32[1,4,128,2048]{3,1,0,2:T(4,128)} %bitcast.118), calls=%async_computation | async-start | bytes 8388608 | tf_op jit(solution)/shard_map/all_to_all | solution.py:102
  308.3 0.0 copy-done.9
  308.3 94.6 %all-to-all-done = f32[1,4,128,2048]{3,1,0,2:T(4,128)} async-done(((f32[1,4,128,2048]{3,1,0,2:T(4,128)}), f32[1,4,128,2048]{3,1,0,2:T(4,128)}, u32[]{:S(2)}, u32[]{:S(2)}) %all-to-all-start) | async-done | bytes 4194336 | tf_op jit(solution)/shard_map/all_to_all | solution.py:102
  402.9 6.6 %copy.51 = f32[1,4,4,32,2048]{4,3,1,2,0:T(8,128)} copy(f32[1,4,4,32,2048]{4,1,3,2,0:T(4,128)} %bitcast.11) | data formatting | bytes 8388608 | tf_op jit(solution)/shard_map/all_to_all | solution.py:102
  409.5 5.0 %gather_fusion = f32[4,4,32,2048]{3,2,1,0:T(8,128)} fusion(f32[4,4,32,2048]{3,2,1,0:T(8,128)} %bitcast.119, s32[1024]{0:T(1024)S(1)} %pad_clamp_fusion), kind=kCustom, calls=%fused_computation | custom fusion | bytes 8388624 | tf_op jit(solution)/shard_map/jit(_take)/gather | solution.py:74
  414.4 4.9 %broadcast_select_fusion.2 = f32[4,4,32,2048]{3,2,1,0:T(8,128)} fusion(f32[4,4,32,2048]{3,2,1,0:T(8,128)} %gather_fusion, pred[4]{0:T(512)(128)(4,1)S(1)} %compare_and_fusion), kind=kLoop, calls=%fused_computation.39 | loop fusion | flops 1048576 | bytes 8388612 | tf_op jit(solution)/shard_map/jit(_take)/select_n | solution.py:74
  419.3 10.6 %while.28 = (s32[]{:T(128)}, f32[32,2048]{1,0:T(8,128)S(1)}, f32[4,32,2048]{2,1,0:T(8,128)S(1)}, f32[4,4,32,2048]{3,2,1,0:T(8,128)}, s32[]{:T(128)}, /*index=5*/s32[]{:T(128)}, s32[]{}) while((s32[]{:T(128)}, f32[32,2048]{1,0:T(8,128)S(1)}, f32[4,32,2048]{2,1,0:T(8,128)S(1)}, f32[4,4,32,2048]{3,2,1,0:T(8,128)}, s32[]{:T(128)}, ...), condition=%wide.region_9.10_spmd.clone, body=%wide.region_8.9_spmd.clone.sunk | while | flops 983044 | bytes 4456560 | solution.py:85
  419.3 1.0 fusion.26
  420.3 1.6 fusion.27
  422.0 1.0 fusion.26
  423.0 1.6 fusion.27
  424.6 1.0 fusion.26
  425.7 1.6 fusion.27
  427.3 1.0 fusion.26
  428.3 1.6 fusion.27
  430.0 0.0 copy-start.3
  430.0 1.0 copy-done.3
  (6 shorter events, 0.0 us)
Async XLA Ops:
  11.8 4.3 %collective-permute-start = (bf16[18,1,2048]{2,0,1:T(8,128)(2,1)S(1)}, bf16[18,1,2048]{2,0,1:T(8,128)(2,1)S(1)}, u32[]{:S(2)}, u32[]{:S(2)}) collective-permute-start(bf16[18,1,2048]{2,0,1:T(8,128)(2,1)S(1)} %get-tuple-element.371), channel_id=1, source_target_pairs={{0,4},{1,5},{2,6},{3,7},{8,12},{9,13},{10,14},{11,15},{16,20},{17,... | collective-permute-start | bytes 221192 | tf_op jit(solution)/shard_map/ppermute | solution.py:17
  13.1 4.0 collective-permute-start.1
  20.0 4.6 %copy-start.2 = (bf16[18,130,2048]{2,0,1:T(8,128)(2,1)}, bf16[18,130,2048]{2,0,1:T(8,128)(2,1)S(1)}, u32[]{:S(2)}) copy-start(bf16[18,130,2048]{2,0,1:T(8,128)(2,1)S(1)} %pad_maximum_fusion.1) | copy-start | bytes 28753924
  25.7 18.5 %collective-permute-start.2 = (bf16[18,130,1]{1,0,2:T(8,128)(2,1)S(1)}, bf16[18,130,1]{1,0,2:T(8,128)(2,1)S(1)}, u32[]{:S(2)}, u32[]{:S(2)}) collective-permute-start(bf16[18,130,1]{1,0,2:T(8,128)(2,1)S(1)} %copy.37), channel_id=1, source_target_pairs={{0,1},{1,2},{2,3},{4,5},{5,6},{6,7},{8,9},{9,10},{10,11},{12,13},{... | collective-permute-start | bytes 14048 | tf_op jit(solution)/shard_map/ppermute | solution.py:17
  29.5 15.1 %collective-permute-start.3 = (bf16[18,130,1]{1,0,2:T(8,128)(2,1)S(1)}, bf16[18,130,1]{1,0,2:T(8,128)(2,1)S(1)}, u32[]{:S(2)}, u32[]{:S(2)}) collective-permute-start(bf16[18,130,1]{1,0,2:T(8,128)(2,1)S(1)} %copy.38), channel_id=1, source_target_pairs={{1,0},{2,1},{3,2},{5,4},{6,5},{7,6},{9,8},{10,9},{11,10},{13,12},{... | collective-permute-start | bytes 14048 | tf_op jit(solution)/shard_map/ppermute | solution.py:18
  45.0 19.3 %copy-start.7 = (f32[4]{0:T(128)S(1)}, f32[4]{0:T(128)}, u32[]{:S(2)}) copy-start(f32[4]{0:T(128)} %param.18) | copy-start | bytes 52
  45.0 19.2 %copy-start.8 = (f32[3]{0:T(128)S(1)}, f32[3]{0:T(128)}, u32[]{:S(2)}) copy-start(f32[3]{0:T(128)} %param.21) | copy-start | bytes 40
  66.8 241.5 %copy-start.9 = (s32[4]{0:T(128)S(1)}, s32[4]{0:T(128)}, u32[]{:S(2)}) copy-start(s32[4]{0:T(128)} %param.15) | copy-start | bytes 52
  73.6 329.2 %all-to-all-start = ((f32[1,4,128,2048]{3,1,0,2:T(4,128)}), f32[1,4,128,2048]{3,1,0,2:T(4,128)}, u32[]{:S(2)}, u32[]{:S(2)}) async-start(f32[1,4,128,2048]{3,1,0,2:T(4,128)} %bitcast.118), calls=%async_computation | async-start | bytes 8388608 | tf_op jit(solution)/shard_map/all_to_all | solution.py:102
  430.0 1.0 copy-start.3
where the time goes:
time: 438 us; the launch traced here: 431 us
  starting transfers between devices  245 us (56%)
  waiting for transfers between devices  95.5 us (22%)
  local copies, waits for them, and re-layouts  71 us (16%)
  other arithmetic  18.4 us (4%)
    all_to_all x1, starting transfers between devices, per_device(): lax.all_to_all(layer_image[None], 'depth', split_axis=2, concat_axis=0, t...  235 us
    all_to_all x1, waiting for transfers between devices, per_device(): lax.all_to_all(layer_image[None], 'depth', split_axis=2, concat_axis=0, t...  94.6 us
    concatenate x2, local copies, waits for them, and re-layouts, with_halo(): x = jnp.concatenate([before, x, after], axis=dim)  30.2 us
    unnamed x11, local copies, waits for them, and re-layouts  17.3 us
  transfers between devices with their start and end apart: 5, of which 2 were waited for; matrix products, arithmetic and copies ran while one was open for 3% of the time, Pallas kernels for 0%

commit v1 on v0

--- a/solution.py
+++ b/solution.py
@@ -98,9 +98,13 @@
         return march_brick(padded, bump_center, bump_width, bump_height, bump_color, light_dir)
 
     layer_image = lax.cond(empty[0, 0, 0] == 1, blank_layer, lit_layer)
-    band_rows = composite(
-        lax.all_to_all(layer_image[None], "depth", split_axis=2, concat_axis=0, tiled=True), order
+    cut_thing_for = lambda obj, at_axis, dimension_no: jnp.concatenate(
+        lax.all_to_all(
+            jnp.stack(jnp.split(obj, lax.axis_size("depth"), axis=at_axis)), "depth", 0, 0
+        ),
+        axis=dimension_no,
     )
+    band_rows = composite(cut_thing_for(layer_image[None], 2, 0), order)
     return band_rows[None]
 
 

time: 438 us -> 404 us (0.922); the launches traced: 431 us -> 402 us
  local copies, waits for them, and re-layouts: 71 us -> 55.4 us
  starting transfers between devices: 245 us -> 230 us
    all_to_all x1, starting transfers between devices: 235 us -> 219 us  [per_device(): lax.all_to_all(jnp.stack(jnp.split(obj, lax.axis_size('depth'), axis=at_a...]
    cond x1 -> x0, local copies, waits for them, and re-layouts: 6.87 us -> none  [per_device(): layer_image = lax.cond(empty[0, 0, 0] == 1, blank_layer, lit_layer)]
    all_to_all x1 -> x0, local copies, waits for them, and re-layouts: 6.59 us -> none  [per_device(): lax.all_to_all(layer_image[None], 'depth', split_axis=2, concat_axis=0, t...]
where the time goes in v1:
time: 404 us; the launch traced here: 402 us
  starting transfers between devices  230 us (57%)
  waiting for transfers between devices  95.5 us (24%)
  local copies, waits for them, and re-layouts  55.4 us (14%)
  other arithmetic  20.7 us (5%)
    all_to_all x1, starting transfers between devices, per_device(): lax.all_to_all(jnp.stack(jnp.split(obj, lax.axis_size('depth'), axis=at_a...  219 us
    all_to_all x1, waiting for transfers between devices, per_device(): lax.all_to_all(jnp.stack(jnp.split(obj, lax.axis_size('depth'), axis=at_a...  94.6 us
    concatenate x2, local copies, waits for them, and re-layouts, with_halo(): x = jnp.concatenate([before, x, after], axis=dim)  30.2 us
    unnamed x11, local copies, waits for them, and re-layouts  17.3 us
  transfers between devices with their start and end apart: 5, of which 2 were waited for; matrix products, arithmetic and copies ran while one was open for 3% of the time, Pallas kernels for 0%

profile of v1, /device:TPU:5, one launch (start us, length us, event | category | flops | bytes accessed | tf_op | source)
XLA Modules:
  0.0 402.3 jit_solution(17716807078425363423)
XLA Ops:
  0.0 11.8 %copy.31 = bf16[1,18,128,2048]{3,1,2,0:T(8,128)(2,1)S(1)} copy(bf16[1,18,128,2048]{3,2,1,0:T(8,128)(2,1)} %param.14) | data formatting | bytes 18874368 | tf_op args[0]
  11.8 1.3 collective-permute-start
  13.1 3.0 collective-permute-start.1
  16.1 0.0 collective-permute-done
  16.1 0.9 collective-permute-done.1
  17.1 3.0 pad_maximum_fusion
  20.0 0.0 copy-start.2
  20.1 4.6 %copy-done.2 = bf16[18,130,2048]{2,0,1:T(8,128)(2,1)} copy-done((bf16[18,130,2048]{2,0,1:T(8,128)(2,1)}, bf16[18,130,2048]{2,0,1:T(8,128)(2,1)S(1)}, u32[]{:S(2)}) %copy-start.2) | copy-done | bytes 9584664
  24.6 0.4 fusion.18
  25.1 0.7 copy.25
  25.7 3.1 collective-permute-start.2
  28.9 0.7 copy.26
  29.5 3.1 collective-permute-start.3
  33.3 10.9 %copy.28 = bf16[18,130,2048]{2,1,0:T(8,128)(2,1)} copy(bf16[18,130,2048]{2,0,1:T(8,128)(2,1)} %copy-done.2) | data formatting | bytes 19169280 | tf_op jit(solution)/shard_map/concatenate | solution.py:19
  44.2 0.0 collective-permute-done.2
  44.2 0.4 copy.27
  44.6 0.0 collective-permute-done.3
  44.6 0.4 copy.29
  45.0 0.0 copy-start.7
  45.0 0.0 copy-start.8
  45.0 19.2 %concatenate.14 = bf16[18,130,2050]{2,1,0:T(8,128)(2,1)} concatenate(bf16[18,130,1]{2,1,0:T(8,128)(2,1)S(1)} %copy.27, bf16[18,130,2048]{2,1,0:T(8,128)(2,1)} %copy.28, bf16[18,130,1]{2,1,0:T(8,128)(2,1)S(1)} %copy.29), dimensions={2} | concatenate | bytes 19188000 | tf_op jit(solution)/shard_map/concatenate | solution.py:19
  64.2 0.0 copy-done.7
  64.2 0.0 copy-done.8
  64.2 0.4 conditional.1
  64.2 0.1 stack.51
  64.3 0.1 stack.51.clone
  64.4 0.1 stack.51.clone.1
  64.5 0.1 stack.51.clone.2
  64.6 0.0 copy-start.9
  64.6 2.3 pad_maximum_fusion.1
  66.9 219.3 %all-to-all-start = ((f32[4,1,4,32,2048]{4,3,2,1,0:T(8,128)}), f32[4,1,4,32,2048]{4,3,2,1,0:T(8,128)}, u32[]{:S(2)}, u32[]{:S(2)}) async-start(f32[4,1,4,32,2048]{4,3,2,1,0:T(8,128)} %pad_maximum_fusion.1), calls=%async_computation | async-start | bytes 8388608 | tf_op jit(solution)/shard_map/all_to_all | solution.py:102
  286.2 0.0 copy-done.9
  286.2 94.6 %all-to-all-done = f32[4,1,4,32,2048]{4,3,2,1,0:T(8,128)} async-done(((f32[4,1,4,32,2048]{4,3,2,1,0:T(8,128)}), f32[4,1,4,32,2048]{4,3,2,1,0:T(8,128)}, u32[]{:S(2)}, u32[]{:S(2)}) %all-to-all-start) | async-done | bytes 4194336 | tf_op jit(solution)/shard_map/all_to_all | solution.py:102
  380.8 5.0 %gather_fusion = f32[4,4,32,2048]{3,2,1,0:T(8,128)} fusion(f32[4,4,32,2048]{3,2,1,0:T(8,128)} %bitcast.15, s32[1024]{0:T(1024)S(1)} %pad_clamp_fusion), kind=kCustom, calls=%fused_computation | custom fusion | bytes 8388624 | tf_op jit(solution)/shard_map/jit(_take)/gather | solution.py:74
  385.8 4.9 %broadcast_select_fusion.2 = f32[4,4,32,2048]{3,2,1,0:T(8,128)} fusion(f32[4,4,32,2048]{3,2,1,0:T(8,128)} %gather_fusion, pred[4]{0:T(512)(128)(4,1)S(1)} %compare_and_fusion), kind=kLoop, calls=%fused_computation.42 | loop fusion | flops 1048576 | bytes 8388612 | tf_op jit(solution)/shard_map/jit(_take)/select_n | solution.py:74
  390.7 10.6 %while.31 = (s32[]{:T(128)}, f32[32,2048]{1,0:T(8,128)S(1)}, f32[4,32,2048]{2,1,0:T(8,128)S(1)}, f32[4,4,32,2048]{3,2,1,0:T(8,128)}, s32[]{:T(128)}, /*index=5*/s32[]{:T(128)}, s32[]{}) while((s32[]{:T(128)}, f32[32,2048]{1,0:T(8,128)S(1)}, f32[4,32,2048]{2,1,0:T(8,128)S(1)}, f32[4,4,32,2048]{3,2,1,0:T(8,128)}, s32[]{:T(128)}, ...), condition=%wide.region_9.10_spmd.clone, body=%wide.region_8.9_spmd.clone.sunk | while | flops 983044 | bytes 4456560 | solution.py:85
  390.7 1.0 fusion.26
  391.7 1.6 fusion.27
  393.3 1.0 fusion.26
  394.4 1.6 fusion.27
  396.0 1.0 fusion.26
  397.0 1.6 fusion.27
  398.7 1.0 fusion.26
  399.7 1.6 fusion.27
  401.3 0.0 copy-start.3
  401.3 1.0 copy-done.3
  (6 shorter events, 0.0 us)
Async XLA Ops:
  11.8 4.3 %collective-permute-start = (bf16[18,1,2048]{2,0,1:T(8,128)(2,1)S(1)}, bf16[18,1,2048]{2,0,1:T(8,128)(2,1)S(1)}, u32[]{:S(2)}, u32[]{:S(2)}) collective-permute-start(bf16[18,1,2048]{2,0,1:T(8,128)(2,1)S(1)} %get-tuple-element.392), channel_id=1, source_target_pairs={{0,4},{1,5},{2,6},{3,7},{8,12},{9,13},{10,14},{11,15},{16,20},{17,... | collective-permute-start | bytes 221192 | tf_op jit(solution)/shard_map/ppermute | solution.py:17
  13.1 4.0 collective-permute-start.1
  20.0 4.6 %copy-start.2 = (bf16[18,130,2048]{2,0,1:T(8,128)(2,1)}, bf16[18,130,2048]{2,0,1:T(8,128)(2,1)S(1)}, u32[]{:S(2)}) copy-start(bf16[18,130,2048]{2,0,1:T(8,128)(2,1)S(1)} %pad_maximum_fusion) | copy-start | bytes 28753924
  25.7 18.5 %collective-permute-start.2 = (bf16[18,130,1]{1,0,2:T(8,128)(2,1)S(1)}, bf16[18,130,1]{1,0,2:T(8,128)(2,1)S(1)}, u32[]{:S(2)}, u32[]{:S(2)}) collective-permute-start(bf16[18,130,1]{1,0,2:T(8,128)(2,1)S(1)} %copy.25), channel_id=1, source_target_pairs={{0,1},{1,2},{2,3},{4,5},{5,6},{6,7},{8,9},{9,10},{10,11},{12,13},{... | collective-permute-start | bytes 14048 | tf_op jit(solution)/shard_map/ppermute | solution.py:17
  29.5 15.1 %collective-permute-start.3 = (bf16[18,130,1]{1,0,2:T(8,128)(2,1)S(1)}, bf16[18,130,1]{1,0,2:T(8,128)(2,1)S(1)}, u32[]{:S(2)}, u32[]{:S(2)}) collective-permute-start(bf16[18,130,1]{1,0,2:T(8,128)(2,1)S(1)} %copy.26), channel_id=1, source_target_pairs={{1,0},{2,1},{3,2},{5,4},{6,5},{7,6},{9,8},{10,9},{11,10},{13,12},{... | collective-permute-start | bytes 14048 | tf_op jit(solution)/shard_map/ppermute | solution.py:18
  45.0 19.2 %copy-start.7 = (f32[4]{0:T(128)S(1)}, f32[4]{0:T(128)}, u32[]{:S(2)}) copy-start(f32[4]{0:T(128)} %param.18) | copy-start | bytes 52
  45.0 19.2 %copy-start.8 = (f32[3]{0:T(128)S(1)}, f32[3]{0:T(128)}, u32[]{:S(2)}) copy-start(f32[3]{0:T(128)} %param.21) | copy-start | bytes 40
  64.6 221.5 %copy-start.9 = (s32[4]{0:T(128)S(1)}, s32[4]{0:T(128)}, u32[]{:S(2)}) copy-start(s32[4]{0:T(128)} %param.15) | copy-start | bytes 52
  66.9 313.9 %all-to-all-start = ((f32[4,1,4,32,2048]{4,3,2,1,0:T(8,128)}), f32[4,1,4,32,2048]{4,3,2,1,0:T(8,128)}, u32[]{:S(2)}, u32[]{:S(2)}) async-start(f32[4,1,4,32,2048]{4,3,2,1,0:T(8,128)} %pad_maximum_fusion.1), calls=%async_computation | async-start | bytes 8388608 | tf_op jit(solution)/shard_map/all_to_all | solution.py:102
  401.3 1.0 copy-start.3
